TPU v7x, 32 devices: a whole 2x2x4 slice. The times are simulated.
32 devices in a mesh: parts: 2 (over x), src: 8 (over z, y), tile: 2 (over core).
Axes of the slice: x: 2, y: 2, z: 4, core: 2. Of those that a mesh axis runs over, the one named last changes fastest.
Arguments:
- mask_values: bfloat16 [2048, 512], P(('parts', 'tile')), parts along dimension 0, may hold values from -1 to 1
- target_image: float32 [2048, 512], P(('parts', 'tile')), parts along dimension 0, may hold values from 0 to 1.5
- jones_pupil: float32 [2, 3, 2, 128, 128], replicated, may hold values from -1.7 to 1.7
- polar_states: float32 [4, 2, 2], replicated, may hold values from -3 to 3
- source_weights: float32 [64], P(('parts', 'src')), parts along dimension 0, may hold values from 0.25 to 4
- pupil_offsets: int32 [64, 2], P(('parts', 'src')), parts along dimension 0, may hold values from 0 to 64
- polar_ids: int32 [64], P(('parts', 'src')), parts along dimension 0, may hold values from 0 to 3
Outputs:
- intensity: float32 [4, 512, 512], P(('parts', 'tile'), 'src'), parts along dimension 0
- mask_grad: float32 [4, 512, 512], P(('parts', 'tile'), 'src'), parts along dimension 0
- source_grad: float32 [64], P(('parts', 'src')), parts along dimension 0
There are 2 independent parts, one for each index of `parts`. A program takes and returns all parts, laid end to end along the dimension named above; an argument that names none is the same for every part. Nothing has to cross between parts.
All inputs are finite; a program needn't handle non-finite values.
Results may differ from a plain program's by a relative error of at most 0.018.
Values may be sent and summed in bfloat16 or wider, within the bound.
No kernel may reach another device: no remote copies, remote signals or barrier semaphores. Data moves between devices by JAX's collectives and lax.ppermute only.
A program may use at most 64 MiB of HBM per device.

v0:
```python
import math

import jax
import jax.numpy as jnp
import numpy as np
from jax import lax
from jax.experimental import pallas as pl
from jax.experimental.pallas import tpu as pltpu
from jax.sharding import PartitionSpec as P


AMB = 64
K = 64
GRID = 2 * K
GRAD_SCALE = 32.0
F32 = jnp.float32
BF16 = jnp.bfloat16


def flip(value, axis, mask):
    pairs = [(i, i ^ mask) for i in range(lax.axis_size(axis))]
    return lax.ppermute(value, axis, pairs)


def narrow(table):
    return np.asarray(table, np.float32).astype(jnp.bfloat16)


def split(table):
    high = narrow(table)
    return high, narrow(np.asarray(table, np.float64) - high.astype(np.float64))


def kernel_of_orders(gap):
    orders = np.arange(1, K)
    return (1.0 + 2.0 * np.cos(gap[..., None] * orders).sum(-1)) / GRID


def make_tables(tile_h, tile_w, tiles):
    window = tile_h + 2 * AMB
    two_pi = 2.0 * math.pi
    orders = np.arange(K) - K // 2
    cols = np.arange(tile_w)
    rows = np.arange(window)
    points = np.arange(GRID)
    col = two_pi * np.mod(cols[:, None] * orders[None], tile_w) / tile_w
    row = two_pi * np.mod(orders[:, None] * rows[None], window) / window
    grid = two_pi * np.mod(orders[:, None] * points[None], GRID) / GRID
    cos, sin = np.cos(grid), np.sin(grid)
    col_fwd = np.concatenate([np.cos(col), -np.sin(col)], 1)
    row_fwd = np.concatenate([np.cos(row), np.sin(row)], 0)
    cols_out = np.block([[cos, sin], [-cos, -sin], [-sin, cos], [-sin, cos]])
    rows_out = np.block([[cos.T, -sin.T], [sin.T, cos.T]])
    cols_back = np.block(
        [[cos.T, -sin.T, -sin.T, cos.T], [sin.T, cos.T, cos.T, sin.T]]
    )
    core = np.arange(tile_h) + AMB
    lift_rows = kernel_of_orders(
        two_pi * (core[:, None] / window - points[None] / GRID)
    )
    lift_cols = kernel_of_orders(
        two_pi * (points[:, None] / GRID - cols[None] / tile_w)
    )
    gram = (tile_w / GRID) * lift_rows.T @ lift_rows
    halo = np.stack([row_fwd[:, tile_h + AMB :], row_fwd[:, :AMB]])
    rim = np.zeros((tiles * tile_h, 2 * K))
    rim[tile_h - AMB : tile_h] = row_fwd[:, :AMB].T
    rim[tile_h : tile_h + AMB] = row_fwd[:, tile_h + AMB :].T
    return dict(
        col_fwd=narrow(col_fwd),
        col_fwd_t=narrow(col_fwd.T),
        row_core=narrow(row_fwd[:, AMB : AMB + tile_h]),
        row_halo=narrow(halo),
        cols_out=narrow(cols_out),
        rows_out=narrow(rows_out),
        rows_back=narrow(rows_out.T),
        cols_back=narrow(cols_back),
        lift_rows=narrow(lift_rows),
        lift_rows_t=narrow(lift_rows.T),
        lift_cols=narrow(lift_cols),
        lift_cols_t=narrow(lift_cols.T),
        gram=np.stack(split(gram)),
        core_t=narrow(row_fwd[:, AMB : AMB + tile_h].T),
        rim_t=narrow(rim),
    )


def dot(a, b):
    return jnp.dot(a, b, preferred_element_type=F32)


def halves(value):
    high = value.astype(BF16)
    return high, (value - high.astype(F32)).astype(BF16)


def dot_wide(table, value):
    high, low = halves(value)
    return dot(table, high) + dot(table, low)


def wide_dot(value, table):
    high, low = halves(value)
    return dot(high, table) + dot(low, table)


def lanes(shape):
    return lax.broadcasted_iota(jnp.int32, shape, 1)


def prepare_kernel(
    polar, jones, part, halo, col_fwd, row_core, row_halo, tables, spectrum, *, norm
):
    left = lanes((K, GRID)) < K
    edge = dot(halo[...], col_fwd[...]).astype(BF16)
    whole = dot(row_core[...], part[...]) + dot(row_halo[lax.axis_index("tile")], edge)
    turned = pltpu.roll(whole[K:], K, 1)
    spectrum[...] = norm * (whole[:K] + jnp.where(left, turned, -turned))
    for pol in range(polar.shape[2]):
        ar, br, ai, bi = (polar[n // 2, n % 2, pol] for n in range(4))
        for j in range(3):
            real = jones[2 * j] * ar - jones[6 + 2 * j] * ai
            real += jones[2 * j + 1] * br - jones[6 + 2 * j + 1] * bi
            imag = jones[2 * j] * ai + jones[6 + 2 * j] * ar
            imag += jones[2 * j + 1] * bi + jones[6 + 2 * j + 1] * br
            tables[2 * (3 * pol + j)] = real
            tables[2 * (3 * pol + j) + 1] = pltpu.roll(imag, K, 1)


def fetch(pairs, sems):
    copies = [pltpu.make_async_copy(a, b, sems.at[n]) for n, (a, b) in enumerate(pairs)]
    for copy in copies:
        copy.start()
    return copies


def core_kernel(mask_far, col_far, part, edge, mask, col_fwd, sems):
    copies = fetch([(mask_far, mask), (col_far, col_fwd)], sems)
    for copy in copies:
        copy.wait()
    start = (1 - lax.axis_index("tile")) * (mask.shape[0] - AMB)
    edge[...] = mask[pl.ds(pl.multiple_of(start, AMB), AMB), :]
    part[...] = dot(mask[...], col_fwd[...]).astype(BF16)


def target_kernel(
    target_far, rows_far, cols_far, wanted, target, lift_rows_t, lift_cols_t, sems
):
    pairs = [(target_far, target), (rows_far, lift_rows_t), (cols_far, lift_cols_t)]
    for copy in fetch(pairs, sems):
        copy.wait()
    seen = dot(lift_rows_t[...], target[...].astype(BF16)).astype(BF16)
    wanted[...] = dot(seen, lift_cols_t[...])


def source_kernel(
    known, spectrum, wanted, tables,
    cols_out, rows_out, rows_back, cols_back, gram,
    image_out, grad_out,
    pupils, fields, powers, image, wide, *buffers,
    norm,
):
    each = known.shape[1]
    groups = known.shape[0] // 4
    units, count = fields.shape[:2]
    unit = count // 3
    even, odd = buffers[:3], buffers[3:]
    left = lanes((K, GRID)) < K

    first = spectrum[...]
    second = pltpu.roll(first, K, 1)

    image[...] = jnp.zeros_like(image)

    def value(row, u, s):
        n = u * unit + s
        group = lax.div(n, each)
        return known[4 * group + row, n - group * each]

    def mask_fields(u, buffer):
        for s in range(unit):
            up, side, pol = (value(row, u, s).astype(jnp.int32) for row in (1, 2, 3))
            inside = (lanes((K, GRID)) >= side) & (lanes((K, GRID)) < side + K)
            turn = jnp.where(side == 0, 0, GRID - side)
            for j in range(3):
                real = tables[2 * (3 * pol + j), pl.ds(up, K), :]
                imag = tables[2 * (3 * pol + j) + 1, pl.ds(up, K), :]
                pupil = pltpu.roll(jnp.where(inside, real, imag), turn, 1)
                f = 3 * s + j
                pupils[u, f] = pupil
                buffer[0][f * K : (f + 1) * K] = (pupil * first).astype(BF16)
                buffer[1][f * K : (f + 1) * K] = (pupil * second).astype(BF16)

    def columns(buffer):
        both = jnp.concatenate([buffer[0][...], buffer[1][...]], 1)
        across = dot(both, cols_out[...]).astype(BF16)
        for f in range(count):
            part = across[f * K : (f + 1) * K]
            buffer[2][f, :K] = part[:, :GRID]
            buffer[2][f, K:] = part[:, GRID:]

    def rows(u, buffer):
        rated = None
        for s in range(unit):
            power = None
            for j in range(3):
                f = 3 * s + j
                field = dot(rows_out[...], buffer[2][f])
                fields[u, f] = field.astype(fields.dtype)
                square = field[:GRID] * field[:GRID] + field[GRID:] * field[GRID:]
                power = square if power is None else power + square
            powers[u, s] = power
            power = value(0, u, s) * power
            rated = power if rated is None else rated + power
        image[...] += rated

    last = units - 1
    mask_fields(0, even)
    columns(even)
    mask_fields(1, odd)

    def forward(u):
        rows(u, even)
        columns(odd)
        mask_fields(u + 2, even)
        rows(u + 1, odd)
        columns(even)
        mask_fields(u + 3, odd)

    def forward_pair(i, carry):
        forward(2 * i)
        return carry

    lax.fori_loop(0, units // 2 - 1, forward_pair, 0)
    rows(last - 1, even)
    columns(odd)
    rows(last, odd)

    total = image[...] * (1.0 / (groups * each * K * K))
    image_out[...] = total

    high, low = halves(total)
    rho = dot(gram[0], high) + dot(gram[0], low) + dot(gram[1], high) - wanted[...]
    double = jnp.concatenate([rho, rho], 0).astype(fields.dtype)

    grad_out[K:] = jnp.zeros_like(grad_out[K:])
    wide[...] = jnp.zeros_like(wide)

    def rows_adjoint(u, buffer):
        for f in range(0, count, 2):
            pair = [fields[u, n] * double for n in (f, f + 1)]
            down = dot(rows_back[...], jnp.concatenate(pair, 1).astype(BF16)).astype(BF16)
            for n in (0, 1):
                one = down[:, n * GRID : (n + 1) * GRID]
                buffer[0][(f + n) * K : (f + n + 1) * K] = one[:K]
                buffer[1][(f + n) * K : (f + n + 1) * K] = one[K:]

    def columns_adjoint(u, buffer):
        both = jnp.concatenate([buffer[0][...], buffer[1][...]], 1)
        back = dot(both, cols_back[...])
        plain_sum = None
        cross_sum = None
        for s in range(unit):
            one = None
            two = None
            for j in range(3):
                f = 3 * s + j
                pupil = pupils[u, f]
                part = back[f * K : (f + 1) * K]
                plain = pupil * part[:, :GRID]
                cross = pupil * part[:, GRID:]
                one = plain if one is None else one + plain
                two = cross if two is None else two + cross
            one = value(0, u, s) * one
            two = value(0, u, s) * two
            plain_sum = one if plain_sum is None else plain_sum + one
            cross_sum = two if cross_sum is None else cross_sum + two
        wide[:, :GRID] += plain_sum
        wide[:, GRID:] += cross_sum

    rows_adjoint(0, even)

    def backward(u):
        columns_adjoint(u, even)
        rows_adjoint(u + 1, odd)
        columns_adjoint(u + 1, odd)
        rows_adjoint(u + 2, even)

    def backward_pair(i, carry):
        backward(2 * i)
        return carry

    lax.fori_loop(0, units // 2 - 1, backward_pair, 0)
    columns_adjoint(last - 1, even)
    rows_adjoint(last, odd)
    columns_adjoint(last, odd)

    scale = norm * 2.0 / (groups * each * K * K)
    one = wide[:, :GRID] * scale
    two = wide[:, GRID:] * scale
    real = one + pltpu.roll(one, K, 1)
    imag = two - pltpu.roll(two, K, 1)
    grad_out[:K] = jnp.where(left, real, -imag)
    terms = jnp.zeros((1, GRID), F32)
    for s in range(each):
        power = powers[s // unit, s % unit]
        term = jnp.sum(jnp.sum(rho * power, 0, keepdims=True), 1, keepdims=True)
        terms = jnp.where(lanes((1, GRID)) == s, term * (1.0 / (K * K)), terms)
    grad_out[K : K + 1] = terms


def own(table, start, share):
    return table[pl.ds(pl.multiple_of(start, share), share), :]


def image_kernel(image, lift_rows, lift_cols, out):
    share = out.shape[1]
    rows = dot_wide(own(lift_rows, lax.axis_index("src") * share, share), image[...])
    out[0] = wide_dot(rows, lift_cols[...])


def mask_kernel(mine, theirs, core_t, rim_t, col_fwd_t, out, source_out, *, pixels):
    each = source_out.shape[1]
    share = out.shape[1]
    left = lanes((K, GRID)) < K
    start = lax.axis_index("src") * share
    rows = 0.0
    for ref, table, first in (
        (mine, core_t, start),
        (theirs, rim_t, lax.axis_index("tile") * core_t.shape[0] + start),
    ):
        top = ref[:K]
        turned = pltpu.roll(top, K, 1)
        both = jnp.concatenate([top, jnp.where(left, -turned, turned)], 0)
        rows += dot_wide(own(table, first, share), both)
    out[0] = GRAD_SCALE * wide_dot(rows, col_fwd_t[...])
    terms = mine[K : K + 1] + theirs[K : K + 1]
    source_out[...] = terms[:, :each] * (1.0 / pixels)


def pack_kernel(weight_far, offset_far, state_far, out, weight, offset, state, sems):
    pairs = [(weight_far, weight), (offset_far, offset), (state_far, state)]
    for copy in fetch(pairs, sems):
        copy.wait()
    out[0:1] = weight[...]
    out[1:3] = offset[...].astype(F32)
    out[3:4] = state[...].astype(F32)


FAR = pl.BlockSpec(memory_space=pltpu.HBM)
VM = pl.BlockSpec(memory_space=pltpu.VMEM)
SM = pl.BlockSpec(memory_space=pltpu.SMEM)


def run(kernel, out_shape, scalars, arrays, flops, scratch=(), held=0, far=False):
    outs = out_shape if isinstance(out_shape, tuple) else (out_shape,)
    if far:
        scratch = [pltpu.VMEM(a.shape, a.dtype) for a in arrays]
        scratch.append(pltpu.SemaphoreType.DMA((len(arrays),)))
        arrays = [pltpu.with_memory_space_constraint(a, pltpu.HBM) for a in arrays]
    size = held + sum(a.size * a.dtype.itemsize for a in (*arrays, *outs))
    return pl.pallas_call(
        kernel,
        out_shape=out_shape,
        in_specs=[SM] * len(scalars) + [FAR if far else VM] * len(arrays),
        out_specs=jax.tree.map(lambda _: VM, out_shape),
        scratch_shapes=scratch,
        compiler_params=pltpu.CompilerParams(vmem_limit_bytes=size + (4 << 20)),
        cost_estimate=pl.CostEstimate(flops=flops, bytes_accessed=size, transcendentals=0),
    )(*scalars, *arrays)


def body(mask_values, target_image, jones_pupil, polar_states, source_weights, pupil_offsets, polar_ids):
    tile_h, tile_w = mask_values.shape
    each = source_weights.shape[0]
    groups = lax.axis_size("src")
    tiles = lax.axis_size("tile")
    share = tile_h // groups
    tab = make_tables(tile_h, tile_w, tiles)
    shape = jax.ShapeDtypeStruct

    known = run(
        pack_kernel, shape((4, each), F32), [],
        [source_weights[None], pupil_offsets.T, polar_ids[None]], flops=1, far=True,
    )
    part, edge = run(
        core_kernel, (shape((tile_h, 2 * K), BF16), shape((AMB, tile_w), BF16)),
        [], [mask_values, tab["col_fwd"]], flops=2**27, far=True,
    )
    halo = flip(edge, "tile", 1)
    wanted = run(
        target_kernel, shape((GRID, GRID), F32), [],
        [target_image, tab["lift_rows_t"], tab["lift_cols_t"]],
        flops=2**27, far=True,
    )
    step = 1
    while step < groups:
        theirs = flip(known, "src", step)
        known = jnp.concatenate([known, theirs], 0)
        step *= 2
    pols = polar_states.shape[0]
    norm = 1.0 / math.sqrt((tile_h + 2 * AMB) * tile_w)
    tables, spectrum = run(
        lambda *refs: prepare_kernel(*refs, norm=norm),
        (shape((6 * pols, GRID, GRID), F32), shape((K, GRID), F32)),
        [polar_states.transpose(1, 2, 0)],
        [jones_pupil.reshape(12, GRID, GRID), part, halo]
        + [tab[n] for n in ("col_fwd", "row_core", "row_halo")],
        flops=48 * pols * GRID * GRID,
    )
    unit = each
    units = groups
    count = 3 * unit
    shapes = [
        ((units, count, K, GRID), F32),
        ((units, count, 2 * GRID, GRID), F32 if groups * each <= 64 else BF16),
        ((units, unit, GRID, GRID), F32),
        ((GRID, GRID), F32),
        ((K, 2 * GRID), F32),
    ]
    shapes += 2 * [
        ((count * K, GRID), BF16),
        ((count * K, GRID), BF16),
        ((count, GRID, GRID), BF16),
    ]
    image, grad = run(
        lambda *refs: source_kernel(*refs, norm=norm),
        (shape((GRID, GRID), F32), shape((K + 8, GRID), F32)),
        [known], [spectrum, wanted, tables]
        + [tab[n] for n in ("cols_out", "rows_out", "rows_back", "cols_back", "gram")],
        flops=2**32,
        scratch=[pltpu.VMEM(*s) for s in shapes],
        held=sum(math.prod(s) * jnp.dtype(d).itemsize for s, d in shapes),
    )
    theirs = flip(grad, "tile", 1)
    own_image = run(
        image_kernel, shape((1, share, tile_w), F32), [],
        [image, tab["lift_rows"], tab["lift_cols"]], flops=2**24,
    )
    own_grad, source_grad = run(
        lambda *refs: mask_kernel(*refs, pixels=tiles * tile_h * tile_w),
        (shape((1, share, tile_w), F32), shape((1, each), F32)), [],
        [grad, theirs, tab["core_t"], tab["rim_t"], tab["col_fwd_t"]], flops=2**24,
    )
    return own_image, own_grad, source_grad.reshape(each)


def solution(mesh):
    placed = (
        P(("parts", "tile"), None),
        P(("parts", "tile"), None),
        P(),
        P(),
        P(("parts", "src")),
        P(("parts", "src"), None),
        P(("parts", "src")),
    )
    return jax.shard_map(
        body,
        mesh=mesh,
        in_specs=placed,
        out_specs=(
            P(("parts", "tile"), "src", None),
            P(("parts", "tile"), "src", None),
            P(("parts", "src")),
        ),
        check_vma=False,
    )
```

profile of v0, /device:TPU:0, one launch (start us, length us, event | category | flops | bytes accessed | tf_op | source)
XLA Modules:
  0.0 26.2 jit_solution(18197869488976525911)
XLA Ops:
  0.6 0.0 copy-start.1
  0.6 0.0 copy-start.5
  0.7 0.0 copy-start.8
  0.7 0.8 %shard_map.229 = f32[4,4]{1,0:T(4,128)S(1)} custom-call(f32[1,4]{1,0:T(1,128)} %bitcast.9, s32[2,4]{1,0:T(2,128)} %bitcast.8, s32[1,4]{1,0:T(1,128)} %bitcast.10), custom_call_target="tpu_custom_call" | custom-call | flops 1 | bytes 128 | tf_op jit(solution)/shard_map/pallas_call | solution.py:362
  1.5 0.0 copy-start.10
  1.5 0.0 copy-start.11
  1.5 0.0 copy-start.12
  1.5 0.0 copy-start.13
  1.6 0.0 copy-start.14
  1.6 3.1 %collective-permute-start = (f32[4,4]{1,0:T(4,128)S(1)}, f32[4,4]{1,0:T(4,128)S(1)}, u32[]{:S(2)}, u32[]{:S(2)}) collective-permute-start(f32[4,4]{1,0:T(4,128)S(1)} %shard_map.229), channel_id=1, source_target_pairs={{0,2},{2,0},{4,6},{6,4},{8,10},{10,8},{12,14},{14,12},{1,3},{3,1},... | collective-permute-start | bytes 200 | tf_op jit(solution)/shard_map/ppermute | solution.py:22
  4.6 1.4 %shard_map.230 = (bf16[512,128]{1,0:T(8,128)(2,1)S(1)}, bf16[64,512]{1,0:T(8,128)(2,1)S(1)}) custom-call(bf16[512,512]{1,0:T(8,128)(2,1)} %mask_far.1, bf16[512,128]{1,0:T(8,128)(2,1)} %constant.30.clone.col_far.refs_4_), custom_call_target="tpu_custom_call" | custom-call | flops 134217728 | bytes 851968 | tf_op jit(solution)/shard_map/pallas_call | solution.py:362
  6.0 0.2 collective-permute-done
  6.2 2.1 %collective-permute-start.1 = (f32[8,4]{1,0:T(8,128)S(1)}, f32[8,4]{1,0:T(8,128)S(1)}, u32[]{:S(2)}, u32[]{:S(2)}) collective-permute-start(f32[8,4]{1,0:T(8,128)S(1)} %pad_maximum_fusion.2), channel_id=1, source_target_pairs={{0,4},{2,6},{4,0},{6,2},{8,12},{10,14},{12,8},{14,10},{1,5},{3,7},... | collective-permute-start | bytes 392 | tf_op jit(solution)/shard_map/ppermute | solution.py:22
  8.3 1.6 %collective-permute-done.1 = f32[8,4]{1,0:T(8,128)S(1)} collective-permute-done((f32[8,4]{1,0:T(8,128)S(1)}, f32[8,4]{1,0:T(8,128)S(1)}, u32[]{:S(2)}, u32[]{:S(2)}) %collective-permute-start.1) | collective-permute-done | bytes 160 | tf_op jit(solution)/shard_map/ppermute | solution.py:22
  9.9 3.1 %collective-permute-start.2 = (f32[16,4]{1,0:T(8,128)S(1)}, f32[16,4]{1,0:T(8,128)S(1)}, u32[]{:S(2)}, u32[]{:S(2)}) collective-permute-start(f32[16,4]{1,0:T(8,128)S(1)} %pad_maximum_fusion.1), channel_id=1, source_target_pairs={{0,8},{2,10},{4,12},{6,14},{8,0},{10,2},{12,4},{14,6},{1,9},{3,11}... | collective-permute-start | bytes 776 | tf_op jit(solution)/shard_map/ppermute | solution.py:22
  13.0 1.6 %shard_map.232.refs_2_ = f32[128,128]{1,0:T(8,128)S(1)} custom-call(f32[512,512]{1,0:T(8,128)} %target_far.1, bf16[128,512]{1,0:T(8,128)(2,1)} %constant.31.clone.rows_far, bf16[512,128]{1,0:T(8,128)(2,1)} %constant.32.clone.cols_far), custom_call_target="tpu_custom_call" | custom-call | flops 134217728 | bytes 1376256 | tf_op jit(solution)/shard_map/pallas_call | solution.py:362
  14.8 1.0 %shard_map.231 = (f32[24,128,128]{2,1,0:T(8,128)S(1)}, f32[64,128]{1,0:T(8,128)S(1)}) custom-call(f32[2,2,4]{2,1,0:T(2,128)S(1)} %bitcast.7, f32[12,128,128]{2,1,0:T(8,128)S(1)} %bitcast.6, bf16[512,128]{1,0:T(8,128)(2,1)S(1)} %get-tuple-element.11.refs_2_, bf16[64,512]{1,0:T(8,128)(2,1)S(1)} %collective-permute-done.3.refs_3_, ...), custom_call_target="tpu_custom_call" | custom-call | flops 3145728 | bytes 2883584 | tf_op jit(solution)/shard_map/pallas_call | solution.py:362
  15.9 0.0 copy-start.4
  15.9 0.0 copy-start.2
  16.0 7.9 %shard_map.233 = (f32[128,128]{1,0:T(8,128)S(1)}, f32[72,128]{1,0:T(8,128)S(1)}) custom-call(f32[32,4]{1,0:T(8,128)S(1)} %pad_maximum_fusion.refs_0_, f32[64,128]{1,0:T(8,128)S(1)} %get-tuple-element.13.refs_1_, f32[128,128]{1,0:T(8,128)S(1)} %shard_map.232.refs_2_, f32[24,128,128]{2,1,0:T(8,128)S(1)} %get-tuple-element.14.refs_3_, ...), custom_call_target="tpu_custom_call" | custom-call | flops 4294967296 | bytes 21762048 | tf_op jit(solution)/shard_map/pallas_call | solution.py:362
  23.8 0.1 collective-permute-start.4
  23.9 1.0 %shard_map.234 = f32[1,64,512]{2,1,0:T(8,128)} custom-call(f32[128,128]{1,0:T(8,128)S(1)} %get-tuple-element.15.image, bf16[512,128]{1,0:T(8,128)(2,1)S(1)} %copy-done.3, bf16[128,512]{1,0:T(8,128)(2,1)S(1)} %copy-done.4), custom_call_target="tpu_custom_call" | custom-call | flops 16777216 | bytes 458752 | tf_op jit(solution)/shard_map/pallas_call | solution.py:362
  24.9 0.2 collective-permute-done.4.refs_1_
  25.1 1.1 %shard_map.235 = (f32[1,64,512]{2,1,0:T(8,128)}, f32[1,4]{1,0:T(1,128)}) custom-call(f32[72,128]{1,0:T(8,128)S(1)} %get-tuple-element.16.refs_0_, f32[72,128]{1,0:T(8,128)S(1)} %collective-permute-done.4.refs_1_, bf16[512,128]{1,0:T(8,128)(2,1)S(1)} %copy-done.6, bf16[1024,128]{1,0:T(8,128)(2,1)S(1)} %copy-done.2, bf16[128,512]{1,0:T(8,128)(2,1)S(1)} %copy-done.7), custom_call_target="tpu_custom_call" | custom-call | flops 16777216 | bytes 729104 | tf_op jit(solution)/shard_map/pallas_call | solution.py:362
  (26 shorter events, 0.1 us)
Async XLA Ops:
  0.6 14.1 %copy-start.1 = (bf16[512,128]{1,0:T(8,128)(2,1)S(1)}, bf16[512,128]{1,0:T(8,128)(2,1)}, u32[]{:S(2)}) copy-start(bf16[512,128]{1,0:T(8,128)(2,1)} %constant.30.clone.col_far.refs_4_) | copy-start | bytes 393220
  0.6 14.1 %copy-start.5 = (bf16[128,512]{1,0:T(8,128)(2,1)S(1)}, bf16[128,512]{1,0:T(8,128)(2,1)}, u32[]{:S(2)}) copy-start(bf16[128,512]{1,0:T(8,128)(2,1)} %constant.33.clone.refs_5_) | copy-start | bytes 393220
  0.7 14.1 %copy-start.8 = (bf16[2,128,64]{2,1,0:T(8,128)(2,1)S(1)}, bf16[2,128,64]{2,1,0:T(8,128)(2,1)}, u32[]{:S(2)}) copy-start(bf16[2,128,64]{2,1,0:T(8,128)(2,1)} %constant.34.clone.refs_6_) | copy-start | bytes 98308
  0.7 14.1 %copy-start.9 = (f32[4,2,2]{0,2,1:T(2,128)S(1)}, f32[4,2,2]{0,2,1:T(2,128)}, u32[]{:S(2)}) copy-start(f32[4,2,2]{0,2,1:T(2,128)} %param.25) | copy-start | bytes 196
  0.7 14.1 %copy-start = (f32[2,3,2,128,128]{4,3,2,1,0:T(8,128)S(1)}, f32[2,3,2,128,128]{4,3,2,1,0:T(8,128)}, u32[]{:S(2)}) copy-start(f32[2,3,2,128,128]{4,3,2,1,0:T(8,128)} %param.24) | copy-start | bytes 2359300
  1.5 14.3 %copy-start.10 = (bf16[256,256]{1,0:T(8,128)(2,1)S(1)}, bf16[256,256]{1,0:T(8,128)(2,1)}, u32[]{:S(2)}) copy-start(bf16[256,256]{1,0:T(8,128)(2,1)} %constant.35.clone.refs_4_) | copy-start | bytes 393220
  1.5 14.3 %copy-start.11 = (bf16[256,256]{1,0:T(8,128)(2,1)S(1)}, bf16[256,256]{1,0:T(8,128)(2,1)}, u32[]{:S(2)}) copy-start(bf16[256,256]{1,0:T(8,128)(2,1)} %constant.38.clone.refs_7_) | copy-start | bytes 393220
  1.5 14.3 %copy-start.12 = (bf16[256,128]{1,0:T(8,128)(2,1)S(1)}, bf16[256,128]{1,0:T(8,128)(2,1)}, u32[]{:S(2)}) copy-start(bf16[256,128]{1,0:T(8,128)(2,1)} %constant.36.clone.refs_5_) | copy-start | bytes 196612
  1.5 14.3 %copy-start.13 = (bf16[128,256]{1,0:T(8,128)(2,1)S(1)}, bf16[128,256]{1,0:T(8,128)(2,1)}, u32[]{:S(2)}) copy-start(bf16[128,256]{1,0:T(8,128)(2,1)} %constant.37.clone.refs_6_) | copy-start | bytes 196612
  1.6 14.3 %copy-start.14 = (bf16[2,128,128]{2,1,0:T(8,128)(2,1)S(1)}, bf16[2,128,128]{2,1,0:T(8,128)(2,1)}, u32[]{:S(2)}) copy-start(bf16[2,128,128]{2,1,0:T(8,128)(2,1)} %constant.39.clone.refs_8_) | copy-start | bytes 196612
  1.6 4.6 %collective-permute-start = (f32[4,4]{1,0:T(4,128)S(1)}, f32[4,4]{1,0:T(4,128)S(1)}, u32[]{:S(2)}, u32[]{:S(2)}) collective-permute-start(f32[4,4]{1,0:T(4,128)S(1)} %shard_map.229), channel_id=1, source_target_pairs={{0,2},{2,0},{4,6},{6,4},{8,10},{10,8},{12,14},{14,12},{1,3},{3,1},... | collective-permute-start | bytes 200 | tf_op jit(solution)/shard_map/ppermute | solution.py:22
  6.2 3.7 %collective-permute-start.1 = (f32[8,4]{1,0:T(8,128)S(1)}, f32[8,4]{1,0:T(8,128)S(1)}, u32[]{:S(2)}, u32[]{:S(2)}) collective-permute-start(f32[8,4]{1,0:T(8,128)S(1)} %pad_maximum_fusion.2), channel_id=1, source_target_pairs={{0,4},{2,6},{4,0},{6,2},{8,12},{10,14},{12,8},{14,10},{1,5},{3,7},... | collective-permute-start | bytes 392 | tf_op jit(solution)/shard_map/ppermute | solution.py:22
  8.3 6.4 %collective-permute-start.3 = (bf16[64,512]{1,0:T(8,128)(2,1)S(1)}, bf16[64,512]{1,0:T(8,128)(2,1)S(1)}, u32[]{:S(2)}, u32[]{:S(2)}) collective-permute-start(bf16[64,512]{1,0:T(8,128)(2,1)S(1)} %get-tuple-element.12), channel_id=1, source_target_pairs={{0,1},{1,0},{2,3},{3,2},{4,5},{5,4},{6,7},{7,6},{8,9},{9,8},{10,11... | collective-permute-start | bytes 196616 | tf_op jit(solution)/shard_map/ppermute | solution.py:22
  9.9 4.8 %collective-permute-start.2 = (f32[16,4]{1,0:T(8,128)S(1)}, f32[16,4]{1,0:T(8,128)S(1)}, u32[]{:S(2)}, u32[]{:S(2)}) collective-permute-start(f32[16,4]{1,0:T(8,128)S(1)} %pad_maximum_fusion.1), channel_id=1, source_target_pairs={{0,8},{2,10},{4,12},{6,14},{8,0},{10,2},{12,4},{14,6},{1,9},{3,11}... | collective-permute-start | bytes 776 | tf_op jit(solution)/shard_map/ppermute | solution.py:22
  15.9 8.0 %copy-start.3 = (bf16[512,128]{1,0:T(8,128)(2,1)S(1)}, bf16[512,128]{1,0:T(8,128)(2,1)}, u32[]{:S(2)}) copy-start(bf16[512,128]{1,0:T(8,128)(2,1)} %constant.40.clone.lift_rows) | copy-start | bytes 393220
  15.9 8.0 %copy-start.4 = (bf16[128,512]{1,0:T(8,128)(2,1)S(1)}, bf16[128,512]{1,0:T(8,128)(2,1)}, u32[]{:S(2)}) copy-start(bf16[128,512]{1,0:T(8,128)(2,1)} %constant.41.clone.lift_cols) | copy-start | bytes 393220
  15.9 9.2 %copy-start.2 = (bf16[1024,128]{1,0:T(8,128)(2,1)S(1)}, bf16[1024,128]{1,0:T(8,128)(2,1)}, u32[]{:S(2)}) copy-start(bf16[1024,128]{1,0:T(8,128)(2,1)} %constant.43.clone.refs_3_) | copy-start | bytes 786436
  15.9 9.2 %copy-start.6 = (bf16[512,128]{1,0:T(8,128)(2,1)S(1)}, bf16[512,128]{1,0:T(8,128)(2,1)}, u32[]{:S(2)}) copy-start(bf16[512,128]{1,0:T(8,128)(2,1)} %constant.42.clone.refs_2_) | copy-start | bytes 393220
  15.9 9.2 %copy-start.7 = (bf16[128,512]{1,0:T(8,128)(2,1)S(1)}, bf16[128,512]{1,0:T(8,128)(2,1)}, u32[]{:S(2)}) copy-start(bf16[128,512]{1,0:T(8,128)(2,1)} %constant.44.clone.refs_4_) | copy-start | bytes 393220
  23.8 1.3 %collective-permute-start.4 = (f32[72,128]{1,0:T(8,128)S(1)}, f32[72,128]{1,0:T(8,128)S(1)}, u32[]{:S(2)}, u32[]{:S(2)}) collective-permute-start(f32[72,128]{1,0:T(8,128)S(1)} %get-tuple-element.16.refs_0_), channel_id=1, source_target_pairs={{0,1},{1,0},{2,3},{3,2},{4,5},{5,4},{6,7},{7,6},{8,9},{9,8},{10,11... | collective-permute-start | bytes 110600 | tf_op jit(solution)/shard_map/ppermute | solution.py:22
where the time goes:
time: 26.4 us; the launch traced here: 26.2 us
  Pallas kernels  14.8 us (56%)
  starting transfers between devices  8.37 us (32%)
  waiting for transfers between devices  1.96 us (7%)
  between operations  0.93 us (4%)
    pallas_call x7, Pallas kernels, run(): pl.pallas_call(kernel, out_shape=out_shape, in_specs=[SM] * len(scalars)...  14.8 us
    ppermute x5, starting transfers between devices, flip(): return lax.ppermute(value, axis, pairs)  8.37 us
    ppermute x5, waiting for transfers between devices, flip(): return lax.ppermute(value, axis, pairs)  1.96 us
  transfers between devices with their start and end apart: 5, of which 3 were waited for; matrix products, arithmetic and copies ran while one was open for 0% of the time, Pallas kernels for 15%

commit v1 on v0

--- a/solution.py
+++ b/solution.py
@@ -153,6 +153,20 @@
     wanted[...] = dot(seen, lift_cols_t[...])
 
 
+def repeat(step, pairs, most):
+    each = most if pairs % most == 0 else 1
+
+    def steps(i, carry):
+        for n in range(each):
+            step(2 * (each * i + n))
+        return carry
+
+    if pairs == each:
+        steps(0, 0)
+    else:
+        lax.fori_loop(0, pairs // each, steps, 0)
+
+
 def source_kernel(
     known, spectrum, wanted, tables,
     cols_out, rows_out, rows_back, cols_back, gram,
@@ -177,65 +191,70 @@
         group = lax.div(n, each)
         return known[4 * group + row, n - group * each]
 
-    def mask_fields(u, buffer):
+    def mask_fields(u, s, buffer):
+        up, side, pol = (value(row, u, s).astype(jnp.int32) for row in (1, 2, 3))
+        inside = (lanes((K, GRID)) >= side) & (lanes((K, GRID)) < side + K)
+        turn = jnp.where(side == 0, 0, GRID - side)
+        for j in range(3):
+            real = tables[2 * (3 * pol + j), pl.ds(up, K), :]
+            imag = tables[2 * (3 * pol + j) + 1, pl.ds(up, K), :]
+            pupil = pltpu.roll(jnp.where(inside, real, imag), turn, 1)
+            f = 3 * s + j
+            pupils[u, f] = pupil
+            buffer[0][f * K : (f + 1) * K] = (pupil * first).astype(BF16)
+            buffer[1][f * K : (f + 1) * K] = (pupil * second).astype(BF16)
+
+    def columns(s, buffer):
+        part = slice(3 * s * K, 3 * (s + 1) * K)
+        both = jnp.concatenate([buffer[0][part], buffer[1][part]], 1)
+        across = dot(both, cols_out[...]).astype(BF16)
+        for j in range(3):
+            part = across[j * K : (j + 1) * K]
+            buffer[2][3 * s + j, :K] = part[:, :GRID]
+            buffer[2][3 * s + j, K:] = part[:, GRID:]
+
+    def rows(u, s, buffer):
+        power = None
+        for j in range(3):
+            f = 3 * s + j
+            field = dot(rows_out[...], buffer[2][f])
+            fields[u, f] = field.astype(fields.dtype)
+            square = field[:GRID] * field[:GRID] + field[GRID:] * field[GRID:]
+            power = square if power is None else power + square
+        powers[u, s] = power
+
+    last = units - 1
+    for s in range(unit):
+        mask_fields(0, s, even)
+    for s in range(unit):
+        columns(s, even)
+        mask_fields(1, s, odd)
+
+    def forward(u):
         for s in range(unit):
-            up, side, pol = (value(row, u, s).astype(jnp.int32) for row in (1, 2, 3))
-            inside = (lanes((K, GRID)) >= side) & (lanes((K, GRID)) < side + K)
-            turn = jnp.where(side == 0, 0, GRID - side)
-            for j in range(3):
-                real = tables[2 * (3 * pol + j), pl.ds(up, K), :]
-                imag = tables[2 * (3 * pol + j) + 1, pl.ds(up, K), :]
-                pupil = pltpu.roll(jnp.where(inside, real, imag), turn, 1)
-                f = 3 * s + j
-                pupils[u, f] = pupil
-                buffer[0][f * K : (f + 1) * K] = (pupil * first).astype(BF16)
-                buffer[1][f * K : (f + 1) * K] = (pupil * second).astype(BF16)
-
-    def columns(buffer):
-        both = jnp.concatenate([buffer[0][...], buffer[1][...]], 1)
-        across = dot(both, cols_out[...]).astype(BF16)
-        for f in range(count):
-            part = across[f * K : (f + 1) * K]
-            buffer[2][f, :K] = part[:, :GRID]
-            buffer[2][f, K:] = part[:, GRID:]
-
-    def rows(u, buffer):
-        rated = None
+            columns(s, odd)
+            rows(u, s, even)
+            mask_fields(u + 2, s, even)
         for s in range(unit):
-            power = None
-            for j in range(3):
-                f = 3 * s + j
-                field = dot(rows_out[...], buffer[2][f])
-                fields[u, f] = field.astype(fields.dtype)
-                square = field[:GRID] * field[:GRID] + field[GRID:] * field[GRID:]
-                power = square if power is None else power + square
-            powers[u, s] = power
-            power = value(0, u, s) * power
-            rated = power if rated is None else rated + power
+            columns(s, even)
+            rows(u + 1, s, odd)
+            mask_fields(u + 3, s, odd)
+
+    repeat(forward, units // 2 - 1, 3)
+    for s in range(unit):
+        columns(s, odd)
+        rows(last - 1, s, even)
+    for s in range(unit):
+        rows(last, s, odd)
+
+    def gather(u, carry):
+        rated = value(0, u, 0) * powers[u, 0]
+        for s in range(1, unit):
+            rated += value(0, u, s) * powers[u, s]
         image[...] += rated
-
-    last = units - 1
-    mask_fields(0, even)
-    columns(even)
-    mask_fields(1, odd)
-
-    def forward(u):
-        rows(u, even)
-        columns(odd)
-        mask_fields(u + 2, even)
-        rows(u + 1, odd)
-        columns(even)
-        mask_fields(u + 3, odd)
-
-    def forward_pair(i, carry):
-        forward(2 * i)
         return carry
 
-    lax.fori_loop(0, units // 2 - 1, forward_pair, 0)
-    rows(last - 1, even)
-    columns(odd)
-    rows(last, odd)
-
+    lax.fori_loop(0, units, gather, 0)
     total = image[...] * (1.0 / (groups * each * K * K))
     image_out[...] = total
 
@@ -246,8 +265,8 @@
     grad_out[K:] = jnp.zeros_like(grad_out[K:])
     wide[...] = jnp.zeros_like(wide)
 
-    def rows_adjoint(u, buffer):
-        for f in range(0, count, 2):
+    def rows_adjoint(u, h, buffer):
+        for f in range(6 * h, 6 * h + 6, 2):
             pair = [fields[u, n] * double for n in (f, f + 1)]
             down = dot(rows_back[...], jnp.concatenate(pair, 1).astype(BF16)).astype(BF16)
             for n in (0, 1):
@@ -255,45 +274,42 @@
                 buffer[0][(f + n) * K : (f + n + 1) * K] = one[:K]
                 buffer[1][(f + n) * K : (f + n + 1) * K] = one[K:]
 
-    def columns_adjoint(u, buffer):
-        both = jnp.concatenate([buffer[0][...], buffer[1][...]], 1)
+    def columns_adjoint(u, h, buffer):
+        part = slice(6 * h * K, 6 * (h + 1) * K)
+        both = jnp.concatenate([buffer[0][part], buffer[1][part]], 1)
         back = dot(both, cols_back[...])
-        plain_sum = None
-        cross_sum = None
-        for s in range(unit):
+        for s in (2 * h, 2 * h + 1):
             one = None
             two = None
             for j in range(3):
-                f = 3 * s + j
-                pupil = pupils[u, f]
+                f = 3 * s + j - 6 * h
+                pupil = pupils[u, 3 * s + j]
                 part = back[f * K : (f + 1) * K]
                 plain = pupil * part[:, :GRID]
                 cross = pupil * part[:, GRID:]
                 one = plain if one is None else one + plain
                 two = cross if two is None else two + cross
-            one = value(0, u, s) * one
-            two = value(0, u, s) * two
-            plain_sum = one if plain_sum is None else plain_sum + one
-            cross_sum = two if cross_sum is None else cross_sum + two
-        wide[:, :GRID] += plain_sum
-        wide[:, GRID:] += cross_sum
-
-    rows_adjoint(0, even)
+            wide[:, :GRID] += value(0, u, s) * one
+            wide[:, GRID:] += value(0, u, s) * two
+
+    two_each = range(unit // 2)
+    for h in two_each:
+        rows_adjoint(0, h, even)
 
     def backward(u):
-        columns_adjoint(u, even)
-        rows_adjoint(u + 1, odd)
-        columns_adjoint(u + 1, odd)
-        rows_adjoint(u + 2, even)
-
-    def backward_pair(i, carry):
-        backward(2 * i)
-        return carry
-
-    lax.fori_loop(0, units // 2 - 1, backward_pair, 0)
-    columns_adjoint(last - 1, even)
-    rows_adjoint(last, odd)
-    columns_adjoint(last, odd)
+        for h in two_each:
+            columns_adjoint(u, h, even)
+            rows_adjoint(u + 1, h, odd)
+        for h in two_each:
+            columns_adjoint(u + 1, h, odd)
+            rows_adjoint(u + 2, h, even)
+
+    repeat(backward, units // 2 - 1, 3)
+    for h in two_each:
+        columns_adjoint(last - 1, h, even)
+        rows_adjoint(last, h, odd)
+    for h in two_each:
+        columns_adjoint(last, h, odd)
 
     scale = norm * 2.0 / (groups * each * K * K)
     one = wide[:, :GRID] * scale

time: 26.4 us -> 25.3 us (0.958)
  Pallas kernels: 14.8 us -> 13.8 us
    pallas_call x7, Pallas kernels: 14.8 us -> 13.8 us  [run(): pl.pallas_call(kernel, out_shape=out_shape, in_specs=[SM] * len(scalars)...]
  transfers between devices with their start and end apart: 5 -> 5, of which waited for: 3 -> 3; matrix products, arithmetic and copies ran while one was open for 0% -> 0% of each run, Pallas kernels for 15% -> 16%
where the time goes in v1:
time: 25.3 us; the launch traced here: 25.2 us
  Pallas kernels  13.8 us (55%)
  starting transfers between devices  8.37 us (33%)
  waiting for transfers between devices  1.96 us (8%)
  between operations  0.93 us (4%)
    pallas_call x7, Pallas kernels, run(): pl.pallas_call(kernel, out_shape=out_shape, in_specs=[SM] * len(scalars)...  13.8 us
    ppermute x5, starting transfers between devices, flip(): return lax.ppermute(value, axis, pairs)  8.37 us
    ppermute x5, waiting for transfers between devices, flip(): return lax.ppermute(value, axis, pairs)  1.96 us
  transfers between devices with their start and end apart: 5, of which 3 were waited for; matrix products, arithmetic and copies ran while one was open for 0% of the time, Pallas kernels for 16%

profile of v1, /device:TPU:0, one launch (start us, length us, event | category | flops | bytes accessed | tf_op | source)
XLA Modules:
  0.0 25.2 jit_solution(15869458380066042541)
XLA Ops:
  0.6 0.0 copy-start.1
  0.6 0.0 copy-start.5
  0.7 0.0 copy-start.8
  0.7 0.8 %shard_map.229 = f32[4,4]{1,0:T(4,128)S(1)} custom-call(f32[1,4]{1,0:T(1,128)} %bitcast.9, s32[2,4]{1,0:T(2,128)} %bitcast.8, s32[1,4]{1,0:T(1,128)} %bitcast.10), custom_call_target="tpu_custom_call" | custom-call | flops 1 | bytes 128 | tf_op jit(solution)/shard_map/pallas_call | solution.py:378
  1.5 0.0 copy-start.10
  1.5 0.0 copy-start.11
  1.5 0.0 copy-start.12
  1.5 0.0 copy-start.13
  1.6 0.0 copy-start.14
  1.6 3.1 %collective-permute-start = (f32[4,4]{1,0:T(4,128)S(1)}, f32[4,4]{1,0:T(4,128)S(1)}, u32[]{:S(2)}, u32[]{:S(2)}) collective-permute-start(f32[4,4]{1,0:T(4,128)S(1)} %shard_map.229), channel_id=1, source_target_pairs={{0,2},{2,0},{4,6},{6,4},{8,10},{10,8},{12,14},{14,12},{1,3},{3,1},... | collective-permute-start | bytes 200 | tf_op jit(solution)/shard_map/ppermute | solution.py:22
  4.6 1.4 %shard_map.230 = (bf16[512,128]{1,0:T(8,128)(2,1)S(1)}, bf16[64,512]{1,0:T(8,128)(2,1)S(1)}) custom-call(bf16[512,512]{1,0:T(8,128)(2,1)} %mask_far.1, bf16[512,128]{1,0:T(8,128)(2,1)} %constant.30.clone.col_far.refs_4_), custom_call_target="tpu_custom_call" | custom-call | flops 134217728 | bytes 851968 | tf_op jit(solution)/shard_map/pallas_call | solution.py:378
  6.0 0.2 collective-permute-done
  6.2 2.1 %collective-permute-start.1 = (f32[8,4]{1,0:T(8,128)S(1)}, f32[8,4]{1,0:T(8,128)S(1)}, u32[]{:S(2)}, u32[]{:S(2)}) collective-permute-start(f32[8,4]{1,0:T(8,128)S(1)} %pad_maximum_fusion.2), channel_id=1, source_target_pairs={{0,4},{2,6},{4,0},{6,2},{8,12},{10,14},{12,8},{14,10},{1,5},{3,7},... | collective-permute-start | bytes 392 | tf_op jit(solution)/shard_map/ppermute | solution.py:22
  8.3 1.6 %collective-permute-done.1 = f32[8,4]{1,0:T(8,128)S(1)} collective-permute-done((f32[8,4]{1,0:T(8,128)S(1)}, f32[8,4]{1,0:T(8,128)S(1)}, u32[]{:S(2)}, u32[]{:S(2)}) %collective-permute-start.1) | collective-permute-done | bytes 160 | tf_op jit(solution)/shard_map/ppermute | solution.py:22
  9.9 3.1 %collective-permute-start.2 = (f32[16,4]{1,0:T(8,128)S(1)}, f32[16,4]{1,0:T(8,128)S(1)}, u32[]{:S(2)}, u32[]{:S(2)}) collective-permute-start(f32[16,4]{1,0:T(8,128)S(1)} %pad_maximum_fusion.1), channel_id=1, source_target_pairs={{0,8},{2,10},{4,12},{6,14},{8,0},{10,2},{12,4},{14,6},{1,9},{3,11}... | collective-permute-start | bytes 776 | tf_op jit(solution)/shard_map/ppermute | solution.py:22
  13.0 1.6 %shard_map.232.refs_2_ = f32[128,128]{1,0:T(8,128)S(1)} custom-call(f32[512,512]{1,0:T(8,128)} %target_far.1, bf16[128,512]{1,0:T(8,128)(2,1)} %constant.31.clone.rows_far, bf16[512,128]{1,0:T(8,128)(2,1)} %constant.32.clone.cols_far), custom_call_target="tpu_custom_call" | custom-call | flops 134217728 | bytes 1376256 | tf_op jit(solution)/shard_map/pallas_call | solution.py:378
  14.8 1.0 %shard_map.231 = (f32[24,128,128]{2,1,0:T(8,128)S(1)}, f32[64,128]{1,0:T(8,128)S(1)}) custom-call(f32[2,2,4]{2,1,0:T(2,128)S(1)} %bitcast.7, f32[12,128,128]{2,1,0:T(8,128)S(1)} %bitcast.6, bf16[512,128]{1,0:T(8,128)(2,1)S(1)} %get-tuple-element.11.refs_2_, bf16[64,512]{1,0:T(8,128)(2,1)S(1)} %collective-permute-done.3.refs_3_, ...), custom_call_target="tpu_custom_call" | custom-call | flops 3145728 | bytes 2883584 | tf_op jit(solution)/shard_map/pallas_call | solution.py:378
  15.9 0.0 copy-start.4
  15.9 0.0 copy-start.2
  16.0 6.8 %shard_map.233 = (f32[128,128]{1,0:T(8,128)S(1)}, f32[72,128]{1,0:T(8,128)S(1)}) custom-call(f32[32,4]{1,0:T(8,128)S(1)} %pad_maximum_fusion.refs_0_, f32[64,128]{1,0:T(8,128)S(1)} %get-tuple-element.13.refs_1_, f32[128,128]{1,0:T(8,128)S(1)} %shard_map.232.refs_2_, f32[24,128,128]{2,1,0:T(8,128)S(1)} %get-tuple-element.14.refs_3_, ...), custom_call_target="tpu_custom_call" | custom-call | flops 4294967296 | bytes 21762048 | tf_op jit(solution)/shard_map/pallas_call | solution.py:378
  22.8 0.1 collective-permute-start.4
  22.9 1.0 %shard_map.234 = f32[1,64,512]{2,1,0:T(8,128)} custom-call(f32[128,128]{1,0:T(8,128)S(1)} %get-tuple-element.15.image, bf16[512,128]{1,0:T(8,128)(2,1)S(1)} %copy-done.3, bf16[128,512]{1,0:T(8,128)(2,1)S(1)} %copy-done.4), custom_call_target="tpu_custom_call" | custom-call | flops 16777216 | bytes 458752 | tf_op jit(solution)/shard_map/pallas_call | solution.py:378
  23.9 0.2 collective-permute-done.4.refs_1_
  24.1 1.1 %shard_map.235 = (f32[1,64,512]{2,1,0:T(8,128)}, f32[1,4]{1,0:T(1,128)}) custom-call(f32[72,128]{1,0:T(8,128)S(1)} %get-tuple-element.16.refs_0_, f32[72,128]{1,0:T(8,128)S(1)} %collective-permute-done.4.refs_1_, bf16[512,128]{1,0:T(8,128)(2,1)S(1)} %copy-done.6, bf16[1024,128]{1,0:T(8,128)(2,1)S(1)} %copy-done.2, bf16[128,512]{1,0:T(8,128)(2,1)S(1)} %copy-done.7), custom_call_target="tpu_custom_call" | custom-call | flops 16777216 | bytes 729104 | tf_op jit(solution)/shard_map/pallas_call | solution.py:378
  (26 shorter events, 0.1 us)
Async XLA Ops:
  0.6 14.1 %copy-start.1 = (bf16[512,128]{1,0:T(8,128)(2,1)S(1)}, bf16[512,128]{1,0:T(8,128)(2,1)}, u32[]{:S(2)}) copy-start(bf16[512,128]{1,0:T(8,128)(2,1)} %constant.30.clone.col_far.refs_4_) | copy-start | bytes 393220
  0.6 14.1 %copy-start.5 = (bf16[128,512]{1,0:T(8,128)(2,1)S(1)}, bf16[128,512]{1,0:T(8,128)(2,1)}, u32[]{:S(2)}) copy-start(bf16[128,512]{1,0:T(8,128)(2,1)} %constant.33.clone.refs_5_) | copy-start | bytes 393220
  0.7 14.1 %copy-start.8 = (bf16[2,128,64]{2,1,0:T(8,128)(2,1)S(1)}, bf16[2,128,64]{2,1,0:T(8,128)(2,1)}, u32[]{:S(2)}) copy-start(bf16[2,128,64]{2,1,0:T(8,128)(2,1)} %constant.34.clone.refs_6_) | copy-start | bytes 98308
  0.7 14.1 %copy-start.9 = (f32[4,2,2]{0,2,1:T(2,128)S(1)}, f32[4,2,2]{0,2,1:T(2,128)}, u32[]{:S(2)}) copy-start(f32[4,2,2]{0,2,1:T(2,128)} %param.25) | copy-start | bytes 196
  0.7 14.1 %copy-start = (f32[2,3,2,128,128]{4,3,2,1,0:T(8,128)S(1)}, f32[2,3,2,128,128]{4,3,2,1,0:T(8,128)}, u32[]{:S(2)}) copy-start(f32[2,3,2,128,128]{4,3,2,1,0:T(8,128)} %param.24) | copy-start | bytes 2359300
  1.5 14.3 %copy-start.10 = (bf16[256,256]{1,0:T(8,128)(2,1)S(1)}, bf16[256,256]{1,0:T(8,128)(2,1)}, u32[]{:S(2)}) copy-start(bf16[256,256]{1,0:T(8,128)(2,1)} %constant.35.clone.refs_4_) | copy-start | bytes 393220
  1.5 14.3 %copy-start.11 = (bf16[256,256]{1,0:T(8,128)(2,1)S(1)}, bf16[256,256]{1,0:T(8,128)(2,1)}, u32[]{:S(2)}) copy-start(bf16[256,256]{1,0:T(8,128)(2,1)} %constant.38.clone.refs_7_) | copy-start | bytes 393220
  1.5 14.3 %copy-start.12 = (bf16[256,128]{1,0:T(8,128)(2,1)S(1)}, bf16[256,128]{1,0:T(8,128)(2,1)}, u32[]{:S(2)}) copy-start(bf16[256,128]{1,0:T(8,128)(2,1)} %constant.36.clone.refs_5_) | copy-start | bytes 196612
  1.5 14.3 %copy-start.13 = (bf16[128,256]{1,0:T(8,128)(2,1)S(1)}, bf16[128,256]{1,0:T(8,128)(2,1)}, u32[]{:S(2)}) copy-start(bf16[128,256]{1,0:T(8,128)(2,1)} %constant.37.clone.refs_6_) | copy-start | bytes 196612
  1.6 14.3 %copy-start.14 = (bf16[2,128,128]{2,1,0:T(8,128)(2,1)S(1)}, bf16[2,128,128]{2,1,0:T(8,128)(2,1)}, u32[]{:S(2)}) copy-start(bf16[2,128,128]{2,1,0:T(8,128)(2,1)} %constant.39.clone.refs_8_) | copy-start | bytes 196612
  1.6 4.6 %collective-permute-start = (f32[4,4]{1,0:T(4,128)S(1)}, f32[4,4]{1,0:T(4,128)S(1)}, u32[]{:S(2)}, u32[]{:S(2)}) collective-permute-start(f32[4,4]{1,0:T(4,128)S(1)} %shard_map.229), channel_id=1, source_target_pairs={{0,2},{2,0},{4,6},{6,4},{8,10},{10,8},{12,14},{14,12},{1,3},{3,1},... | collective-permute-start | bytes 200 | tf_op jit(solution)/shard_map/ppermute | solution.py:22
  6.2 3.7 %collective-permute-start.1 = (f32[8,4]{1,0:T(8,128)S(1)}, f32[8,4]{1,0:T(8,128)S(1)}, u32[]{:S(2)}, u32[]{:S(2)}) collective-permute-start(f32[8,4]{1,0:T(8,128)S(1)} %pad_maximum_fusion.2), channel_id=1, source_target_pairs={{0,4},{2,6},{4,0},{6,2},{8,12},{10,14},{12,8},{14,10},{1,5},{3,7},... | collective-permute-start | bytes 392 | tf_op jit(solution)/shard_map/ppermute | solution.py:22
  8.3 6.4 %collective-permute-start.3 = (bf16[64,512]{1,0:T(8,128)(2,1)S(1)}, bf16[64,512]{1,0:T(8,128)(2,1)S(1)}, u32[]{:S(2)}, u32[]{:S(2)}) collective-permute-start(bf16[64,512]{1,0:T(8,128)(2,1)S(1)} %get-tuple-element.12), channel_id=1, source_target_pairs={{0,1},{1,0},{2,3},{3,2},{4,5},{5,4},{6,7},{7,6},{8,9},{9,8},{10,11... | collective-permute-start | bytes 196616 | tf_op jit(solution)/shard_map/ppermute | solution.py:22
  9.9 4.8 %collective-permute-start.2 = (f32[16,4]{1,0:T(8,128)S(1)}, f32[16,4]{1,0:T(8,128)S(1)}, u32[]{:S(2)}, u32[]{:S(2)}) collective-permute-start(f32[16,4]{1,0:T(8,128)S(1)} %pad_maximum_fusion.1), channel_id=1, source_target_pairs={{0,8},{2,10},{4,12},{6,14},{8,0},{10,2},{12,4},{14,6},{1,9},{3,11}... | collective-permute-start | bytes 776 | tf_op jit(solution)/shard_map/ppermute | solution.py:22
  15.9 7.0 %copy-start.3 = (bf16[512,128]{1,0:T(8,128)(2,1)S(1)}, bf16[512,128]{1,0:T(8,128)(2,1)}, u32[]{:S(2)}) copy-start(bf16[512,128]{1,0:T(8,128)(2,1)} %constant.40.clone.lift_rows) | copy-start | bytes 393220
  15.9 7.0 %copy-start.4 = (bf16[128,512]{1,0:T(8,128)(2,1)S(1)}, bf16[128,512]{1,0:T(8,128)(2,1)}, u32[]{:S(2)}) copy-start(bf16[128,512]{1,0:T(8,128)(2,1)} %constant.41.clone.lift_cols) | copy-start | bytes 393220
  15.9 8.1 %copy-start.2 = (bf16[1024,128]{1,0:T(8,128)(2,1)S(1)}, bf16[1024,128]{1,0:T(8,128)(2,1)}, u32[]{:S(2)}) copy-start(bf16[1024,128]{1,0:T(8,128)(2,1)} %constant.43.clone.refs_3_) | copy-start | bytes 786436
  15.9 8.1 %copy-start.6 = (bf16[512,128]{1,0:T(8,128)(2,1)S(1)}, bf16[512,128]{1,0:T(8,128)(2,1)}, u32[]{:S(2)}) copy-start(bf16[512,128]{1,0:T(8,128)(2,1)} %constant.42.clone.refs_2_) | copy-start | bytes 393220
  15.9 8.1 %copy-start.7 = (bf16[128,512]{1,0:T(8,128)(2,1)S(1)}, bf16[128,512]{1,0:T(8,128)(2,1)}, u32[]{:S(2)}) copy-start(bf16[128,512]{1,0:T(8,128)(2,1)} %constant.44.clone.refs_4_) | copy-start | bytes 393220
  22.8 1.3 %collective-permute-start.4 = (f32[72,128]{1,0:T(8,128)S(1)}, f32[72,128]{1,0:T(8,128)S(1)}, u32[]{:S(2)}, u32[]{:S(2)}) collective-permute-start(f32[72,128]{1,0:T(8,128)S(1)} %get-tuple-element.16.refs_0_), channel_id=1, source_target_pairs={{0,1},{1,0},{2,3},{3,2},{4,5},{5,4},{6,7},{7,6},{8,9},{9,8},{10,11... | collective-permute-start | bytes 110600 | tf_op jit(solution)/shard_map/ppermute | solution.py:22

commit v2 on v1

--- a/solution.py
+++ b/solution.py
@@ -171,7 +171,7 @@
     known, spectrum, wanted, tables,
     cols_out, rows_out, rows_back, cols_back, gram,
     image_out, grad_out,
-    pupils, fields, powers, image, wide, *buffers,
+    pupils, fields, powers, wide, *buffers,
     norm,
 ):
     each = known.shape[1]
@@ -183,8 +183,6 @@
 
     first = spectrum[...]
     second = pltpu.roll(first, K, 1)
-
-    image[...] = jnp.zeros_like(image)
 
     def value(row, u, s):
         n = u * unit + s
@@ -247,15 +245,15 @@
     for s in range(unit):
         rows(last, s, odd)
 
-    def gather(u, carry):
-        rated = value(0, u, 0) * powers[u, 0]
-        for s in range(1, unit):
-            rated += value(0, u, s) * powers[u, s]
-        image[...] += rated
-        return carry
-
-    lax.fori_loop(0, units, gather, 0)
-    total = image[...] * (1.0 / (groups * each * K * K))
+    def gather(i, rated):
+        for n in range(2):
+            u = 2 * i + n
+            for s in range(unit):
+                rated += value(0, u, s) * powers[u, s]
+        return rated
+
+    rated = lax.fori_loop(0, units // 2, gather, jnp.zeros((GRID, GRID), F32))
+    total = rated * (1.0 / (groups * each * K * K))
     image_out[...] = total
 
     high, low = halves(total)
@@ -431,7 +429,6 @@
         ((units, count, K, GRID), F32),
         ((units, count, 2 * GRID, GRID), F32 if groups * each <= 64 else BF16),
         ((units, unit, GRID, GRID), F32),
-        ((GRID, GRID), F32),
         ((K, 2 * GRID), F32),
     ]
     shapes += 2 * [

time: 25.3 us -> 25.3 us (level)
  no operation moved by 1% of the time
where the time goes in v2:
time: 25.3 us; the launch traced here: 25.1 us
  Pallas kernels  13.7 us (54%)
  starting transfers between devices  8.37 us (33%)
  waiting for transfers between devices  1.96 us (8%)
  between operations  0.93 us (4%)
    pallas_call x7, Pallas kernels, run(): pl.pallas_call(kernel, out_shape=out_shape, in_specs=[SM] * len(scalars)...  13.7 us
    ppermute x5, starting transfers between devices, flip(): return lax.ppermute(value, axis, pairs)  8.37 us
    ppermute x5, waiting for transfers between devices, flip(): return lax.ppermute(value, axis, pairs)  1.96 us
  transfers between devices with their start and end apart: 5, of which 3 were waited for; matrix products, arithmetic and copies ran while one was open for 0% of the time, Pallas kernels for 16%

profile of v2, /device:TPU:0, one launch (start us, length us, event | category | flops | bytes accessed | tf_op | source)
XLA Modules:
  0.0 25.1 jit_solution(3250751156037788740)
XLA Ops:
  0.6 0.0 copy-start.1
  0.6 0.0 copy-start.5
  0.7 0.0 copy-start.8
  0.7 0.8 %shard_map.229 = f32[4,4]{1,0:T(4,128)S(1)} custom-call(f32[1,4]{1,0:T(1,128)} %bitcast.9, s32[2,4]{1,0:T(2,128)} %bitcast.8, s32[1,4]{1,0:T(1,128)} %bitcast.10), custom_call_target="tpu_custom_call" | custom-call | flops 1 | bytes 128 | tf_op jit(solution)/shard_map/pallas_call | solution.py:376
  1.5 0.0 copy-start.10
  1.5 0.0 copy-start.11
  1.5 0.0 copy-start.12
  1.5 0.0 copy-start.13
  1.6 0.0 copy-start.14
  1.6 3.1 %collective-permute-start = (f32[4,4]{1,0:T(4,128)S(1)}, f32[4,4]{1,0:T(4,128)S(1)}, u32[]{:S(2)}, u32[]{:S(2)}) collective-permute-start(f32[4,4]{1,0:T(4,128)S(1)} %shard_map.229), channel_id=1, source_target_pairs={{0,2},{2,0},{4,6},{6,4},{8,10},{10,8},{12,14},{14,12},{1,3},{3,1},... | collective-permute-start | bytes 200 | tf_op jit(solution)/shard_map/ppermute | solution.py:22
  4.6 1.4 %shard_map.230 = (bf16[512,128]{1,0:T(8,128)(2,1)S(1)}, bf16[64,512]{1,0:T(8,128)(2,1)S(1)}) custom-call(bf16[512,512]{1,0:T(8,128)(2,1)} %mask_far.1, bf16[512,128]{1,0:T(8,128)(2,1)} %constant.30.clone.col_far.refs_4_), custom_call_target="tpu_custom_call" | custom-call | flops 134217728 | bytes 851968 | tf_op jit(solution)/shard_map/pallas_call | solution.py:376
  6.0 0.2 collective-permute-done
  6.2 2.1 %collective-permute-start.1 = (f32[8,4]{1,0:T(8,128)S(1)}, f32[8,4]{1,0:T(8,128)S(1)}, u32[]{:S(2)}, u32[]{:S(2)}) collective-permute-start(f32[8,4]{1,0:T(8,128)S(1)} %pad_maximum_fusion.2), channel_id=1, source_target_pairs={{0,4},{2,6},{4,0},{6,2},{8,12},{10,14},{12,8},{14,10},{1,5},{3,7},... | collective-permute-start | bytes 392 | tf_op jit(solution)/shard_map/ppermute | solution.py:22
  8.3 1.6 %collective-permute-done.1 = f32[8,4]{1,0:T(8,128)S(1)} collective-permute-done((f32[8,4]{1,0:T(8,128)S(1)}, f32[8,4]{1,0:T(8,128)S(1)}, u32[]{:S(2)}, u32[]{:S(2)}) %collective-permute-start.1) | collective-permute-done | bytes 160 | tf_op jit(solution)/shard_map/ppermute | solution.py:22
  9.9 3.1 %collective-permute-start.2 = (f32[16,4]{1,0:T(8,128)S(1)}, f32[16,4]{1,0:T(8,128)S(1)}, u32[]{:S(2)}, u32[]{:S(2)}) collective-permute-start(f32[16,4]{1,0:T(8,128)S(1)} %pad_maximum_fusion.1), channel_id=1, source_target_pairs={{0,8},{2,10},{4,12},{6,14},{8,0},{10,2},{12,4},{14,6},{1,9},{3,11}... | collective-permute-start | bytes 776 | tf_op jit(solution)/shard_map/ppermute | solution.py:22
  13.0 1.6 %shard_map.232.refs_2_ = f32[128,128]{1,0:T(8,128)S(1)} custom-call(f32[512,512]{1,0:T(8,128)} %target_far.1, bf16[128,512]{1,0:T(8,128)(2,1)} %constant.31.clone.rows_far, bf16[512,128]{1,0:T(8,128)(2,1)} %constant.32.clone.cols_far), custom_call_target="tpu_custom_call" | custom-call | flops 134217728 | bytes 1376256 | tf_op jit(solution)/shard_map/pallas_call | solution.py:376
  14.8 1.0 %shard_map.231 = (f32[24,128,128]{2,1,0:T(8,128)S(1)}, f32[64,128]{1,0:T(8,128)S(1)}) custom-call(f32[2,2,4]{2,1,0:T(2,128)S(1)} %bitcast.7, f32[12,128,128]{2,1,0:T(8,128)S(1)} %bitcast.6, bf16[512,128]{1,0:T(8,128)(2,1)S(1)} %get-tuple-element.11.refs_2_, bf16[64,512]{1,0:T(8,128)(2,1)S(1)} %collective-permute-done.3.refs_3_, ...), custom_call_target="tpu_custom_call" | custom-call | flops 3145728 | bytes 2883584 | tf_op jit(solution)/shard_map/pallas_call | solution.py:376
  15.9 0.0 copy-start.4
  15.9 0.0 copy-start.2
  16.0 6.8 %shard_map.233 = (f32[128,128]{1,0:T(8,128)S(1)}, f32[72,128]{1,0:T(8,128)S(1)}) custom-call(f32[32,4]{1,0:T(8,128)S(1)} %pad_maximum_fusion.refs_0_, f32[64,128]{1,0:T(8,128)S(1)} %get-tuple-element.13.refs_1_, f32[128,128]{1,0:T(8,128)S(1)} %shard_map.232.refs_2_, f32[24,128,128]{2,1,0:T(8,128)S(1)} %get-tuple-element.14.refs_3_, ...), custom_call_target="tpu_custom_call" | custom-call | flops 4294967296 | bytes 21696512 | tf_op jit(solution)/shard_map/pallas_call | solution.py:376
  22.7 0.1 collective-permute-start.4
  22.8 1.0 %shard_map.234 = f32[1,64,512]{2,1,0:T(8,128)} custom-call(f32[128,128]{1,0:T(8,128)S(1)} %get-tuple-element.15.image, bf16[512,128]{1,0:T(8,128)(2,1)S(1)} %copy-done.3, bf16[128,512]{1,0:T(8,128)(2,1)S(1)} %copy-done.4), custom_call_target="tpu_custom_call" | custom-call | flops 16777216 | bytes 458752 | tf_op jit(solution)/shard_map/pallas_call | solution.py:376
  23.8 0.2 collective-permute-done.4.refs_1_
  24.0 1.1 %shard_map.235 = (f32[1,64,512]{2,1,0:T(8,128)}, f32[1,4]{1,0:T(1,128)}) custom-call(f32[72,128]{1,0:T(8,128)S(1)} %get-tuple-element.16.refs_0_, f32[72,128]{1,0:T(8,128)S(1)} %collective-permute-done.4.refs_1_, bf16[512,128]{1,0:T(8,128)(2,1)S(1)} %copy-done.6, bf16[1024,128]{1,0:T(8,128)(2,1)S(1)} %copy-done.2, bf16[128,512]{1,0:T(8,128)(2,1)S(1)} %copy-done.7), custom_call_target="tpu_custom_call" | custom-call | flops 16777216 | bytes 729104 | tf_op jit(solution)/shard_map/pallas_call | solution.py:376
  (26 shorter events, 0.1 us)
Async XLA Ops:
  0.6 14.1 %copy-start.1 = (bf16[512,128]{1,0:T(8,128)(2,1)S(1)}, bf16[512,128]{1,0:T(8,128)(2,1)}, u32[]{:S(2)}) copy-start(bf16[512,128]{1,0:T(8,128)(2,1)} %constant.30.clone.col_far.refs_4_) | copy-start | bytes 393220
  0.6 14.1 %copy-start.5 = (bf16[128,512]{1,0:T(8,128)(2,1)S(1)}, bf16[128,512]{1,0:T(8,128)(2,1)}, u32[]{:S(2)}) copy-start(bf16[128,512]{1,0:T(8,128)(2,1)} %constant.33.clone.refs_5_) | copy-start | bytes 393220
  0.7 14.1 %copy-start.8 = (bf16[2,128,64]{2,1,0:T(8,128)(2,1)S(1)}, bf16[2,128,64]{2,1,0:T(8,128)(2,1)}, u32[]{:S(2)}) copy-start(bf16[2,128,64]{2,1,0:T(8,128)(2,1)} %constant.34.clone.refs_6_) | copy-start | bytes 98308
  0.7 14.1 %copy-start.9 = (f32[4,2,2]{0,2,1:T(2,128)S(1)}, f32[4,2,2]{0,2,1:T(2,128)}, u32[]{:S(2)}) copy-start(f32[4,2,2]{0,2,1:T(2,128)} %param.25) | copy-start | bytes 196
  0.7 14.1 %copy-start = (f32[2,3,2,128,128]{4,3,2,1,0:T(8,128)S(1)}, f32[2,3,2,128,128]{4,3,2,1,0:T(8,128)}, u32[]{:S(2)}) copy-start(f32[2,3,2,128,128]{4,3,2,1,0:T(8,128)} %param.24) | copy-start | bytes 2359300
  1.5 14.3 %copy-start.10 = (bf16[256,256]{1,0:T(8,128)(2,1)S(1)}, bf16[256,256]{1,0:T(8,128)(2,1)}, u32[]{:S(2)}) copy-start(bf16[256,256]{1,0:T(8,128)(2,1)} %constant.35.clone.refs_4_) | copy-start | bytes 393220
  1.5 14.3 %copy-start.11 = (bf16[256,256]{1,0:T(8,128)(2,1)S(1)}, bf16[256,256]{1,0:T(8,128)(2,1)}, u32[]{:S(2)}) copy-start(bf16[256,256]{1,0:T(8,128)(2,1)} %constant.38.clone.refs_7_) | copy-start | bytes 393220
  1.5 14.3 %copy-start.12 = (bf16[256,128]{1,0:T(8,128)(2,1)S(1)}, bf16[256,128]{1,0:T(8,128)(2,1)}, u32[]{:S(2)}) copy-start(bf16[256,128]{1,0:T(8,128)(2,1)} %constant.36.clone.refs_5_) | copy-start | bytes 196612
  1.5 14.3 %copy-start.13 = (bf16[128,256]{1,0:T(8,128)(2,1)S(1)}, bf16[128,256]{1,0:T(8,128)(2,1)}, u32[]{:S(2)}) copy-start(bf16[128,256]{1,0:T(8,128)(2,1)} %constant.37.clone.refs_6_) | copy-start | bytes 196612
  1.6 14.3 %copy-start.14 = (bf16[2,128,128]{2,1,0:T(8,128)(2,1)S(1)}, bf16[2,128,128]{2,1,0:T(8,128)(2,1)}, u32[]{:S(2)}) copy-start(bf16[2,128,128]{2,1,0:T(8,128)(2,1)} %constant.39.clone.refs_8_) | copy-start | bytes 196612
  1.6 4.6 %collective-permute-start = (f32[4,4]{1,0:T(4,128)S(1)}, f32[4,4]{1,0:T(4,128)S(1)}, u32[]{:S(2)}, u32[]{:S(2)}) collective-permute-start(f32[4,4]{1,0:T(4,128)S(1)} %shard_map.229), channel_id=1, source_target_pairs={{0,2},{2,0},{4,6},{6,4},{8,10},{10,8},{12,14},{14,12},{1,3},{3,1},... | collective-permute-start | bytes 200 | tf_op jit(solution)/shard_map/ppermute | solution.py:22
  6.2 3.7 %collective-permute-start.1 = (f32[8,4]{1,0:T(8,128)S(1)}, f32[8,4]{1,0:T(8,128)S(1)}, u32[]{:S(2)}, u32[]{:S(2)}) collective-permute-start(f32[8,4]{1,0:T(8,128)S(1)} %pad_maximum_fusion.2), channel_id=1, source_target_pairs={{0,4},{2,6},{4,0},{6,2},{8,12},{10,14},{12,8},{14,10},{1,5},{3,7},... | collective-permute-start | bytes 392 | tf_op jit(solution)/shard_map/ppermute | solution.py:22
  8.3 6.4 %collective-permute-start.3 = (bf16[64,512]{1,0:T(8,128)(2,1)S(1)}, bf16[64,512]{1,0:T(8,128)(2,1)S(1)}, u32[]{:S(2)}, u32[]{:S(2)}) collective-permute-start(bf16[64,512]{1,0:T(8,128)(2,1)S(1)} %get-tuple-element.12), channel_id=1, source_target_pairs={{0,1},{1,0},{2,3},{3,2},{4,5},{5,4},{6,7},{7,6},{8,9},{9,8},{10,11... | collective-permute-start | bytes 196616 | tf_op jit(solution)/shard_map/ppermute | solution.py:22
  9.9 4.8 %collective-permute-start.2 = (f32[16,4]{1,0:T(8,128)S(1)}, f32[16,4]{1,0:T(8,128)S(1)}, u32[]{:S(2)}, u32[]{:S(2)}) collective-permute-start(f32[16,4]{1,0:T(8,128)S(1)} %pad_maximum_fusion.1), channel_id=1, source_target_pairs={{0,8},{2,10},{4,12},{6,14},{8,0},{10,2},{12,4},{14,6},{1,9},{3,11}... | collective-permute-start | bytes 776 | tf_op jit(solution)/shard_map/ppermute | solution.py:22
  15.9 6.9 %copy-start.3 = (bf16[512,128]{1,0:T(8,128)(2,1)S(1)}, bf16[512,128]{1,0:T(8,128)(2,1)}, u32[]{:S(2)}) copy-start(bf16[512,128]{1,0:T(8,128)(2,1)} %constant.40.clone.lift_rows) | copy-start | bytes 393220
  15.9 6.9 %copy-start.4 = (bf16[128,512]{1,0:T(8,128)(2,1)S(1)}, bf16[128,512]{1,0:T(8,128)(2,1)}, u32[]{:S(2)}) copy-start(bf16[128,512]{1,0:T(8,128)(2,1)} %constant.41.clone.lift_cols) | copy-start | bytes 393220
  15.9 8.1 %copy-start.2 = (bf16[1024,128]{1,0:T(8,128)(2,1)S(1)}, bf16[1024,128]{1,0:T(8,128)(2,1)}, u32[]{:S(2)}) copy-start(bf16[1024,128]{1,0:T(8,128)(2,1)} %constant.43.clone.refs_3_) | copy-start | bytes 786436
  15.9 8.1 %copy-start.6 = (bf16[512,128]{1,0:T(8,128)(2,1)S(1)}, bf16[512,128]{1,0:T(8,128)(2,1)}, u32[]{:S(2)}) copy-start(bf16[512,128]{1,0:T(8,128)(2,1)} %constant.42.clone.refs_2_) | copy-start | bytes 393220
  15.9 8.1 %copy-start.7 = (bf16[128,512]{1,0:T(8,128)(2,1)S(1)}, bf16[128,512]{1,0:T(8,128)(2,1)}, u32[]{:S(2)}) copy-start(bf16[128,512]{1,0:T(8,128)(2,1)} %constant.44.clone.refs_4_) | copy-start | bytes 393220
  22.7 1.3 %collective-permute-start.4 = (f32[72,128]{1,0:T(8,128)S(1)}, f32[72,128]{1,0:T(8,128)S(1)}, u32[]{:S(2)}, u32[]{:S(2)}) collective-permute-start(f32[72,128]{1,0:T(8,128)S(1)} %get-tuple-element.16.refs_0_), channel_id=1, source_target_pairs={{0,1},{1,0},{2,3},{3,2},{4,5},{5,4},{6,7},{7,6},{8,9},{9,8},{10,11... | collective-permute-start | bytes 110600 | tf_op jit(solution)/shard_map/ppermute | solution.py:22
